TPU v7x, 32 devices: a whole 2x2x4 slice. The times are simulated.
32 devices in a mesh: groups: 2 (over y), frame: 4 (over x, core), row: 4 (over z).
Axes of the slice: x: 2, y: 2, z: 4, core: 2. Of those that a mesh axis runs over, the one named last changes fastest.
Arguments:
- observed: float32 [16, 128, 2048], P('frame', ('groups', 'row')), parts along dimension 1, may hold values from 0.5 to 8
- kernels: float32 [8, 5], replicated, may hold values from 0.05 to 1
- band_kernel: int32 [16], P('groups'), parts along dimension 0, may hold values from 0 to 7
- masks: int32 [256, 128, 16], P(None, ('groups', 'row'), 'frame'), parts along dimension 1, may hold values from 0 to 1, as said below
Outputs:
- spikes: bfloat16 [16, 128, 2048], P(None, ('groups', 'row'), 'frame'), parts along dimension 1
- traces: float32 [512, 16], P(('groups', 'frame', 'row')), parts along dimension 0
There are 2 independent parts, one for each index of `groups`. A program takes and returns all parts, laid end to end along the dimension named above; an argument that names none is the same for every part. Nothing has to cross between parts.
Inputs may be any that keep to these rules, and one draw needn't show every extreme that they name: `masks`: each component covers the tile at its centre and a random half of the tiles within 8 rows and one tile column of that centre, so it covers at least one tile.
All inputs are finite; a program needn't handle non-finite values.
Results may differ from a plain program's by a relative error of at most 0.0062.
Values may be sent and summed in bfloat16 or wider, within the bound.
A program may use at most 64 MiB of HBM per device.

v0:
```python
import jax
import jax.numpy as jnp
from jax import lax
from jax.sharding import PartitionSpec as P

TILE = 128
BAND = 8
ITERS = 3
SMOOTHING = 1024.0
DECAY_RATE = 0.9


def padded_2(cells, sides, width):
    for axis, dim in sides:
        count = lax.axis_size(axis)
        ends = count - 1
        head = lax.slice_in_dim(cells, 0, width, axis=dim)
        tail = lax.slice_in_dim(cells, cells.shape[dim] - width, cells.shape[dim], axis=dim)
        cells = jnp.concatenate(
            [
                lax.ppermute(tail, axis, [(i, (i + 1) % count) for i in range(ends)]),
                cells,
                lax.ppermute(head, axis, [((i + 1) % count, i) for i in range(ends)]),
            ],
            axis=dim,
        )
    return cells


def tap_rows(tap_table, band_kernel, first_row, row_count, height):
    row_ids = jnp.clip(first_row + jnp.arange(row_count), 0, height - 1)
    row_bands = row_ids // BAND
    band_slots = jnp.arange(band_kernel.shape[0])
    kernel_ids = jnp.sum(
        jnp.where(row_bands[:, None] == band_slots[None, :], band_kernel[None, :], 0), axis=1
    )
    kernel_slots = jnp.arange(tap_table.shape[0])
    picked = jnp.where(
        kernel_ids[:, None, None] == kernel_slots[None, :, None], tap_table[None, :, :], 0.0
    )
    return jnp.sum(picked, axis=1)


def blur_rows(padded, row_taps, row_count):
    summed = row_taps[:, 0][None, :, None] * padded[:, 0:row_count]
    for offset in range(1, 5):
        summed = (
            summed + row_taps[:, offset][None, :, None] * padded[:, offset : offset + row_count]
        )
    return summed


def back_rows(padded_quotient, outer_taps, row_count):
    summed = outer_taps[4 : 4 + row_count, 0][None, :, None] * padded_quotient[:, 4 : 4 + row_count]
    for offset in range(1, 5):
        start = 4 - offset
        summed = (
            summed
            + outer_taps[start : start + row_count, offset][None, :, None]
            * padded_quotient[:, start : start + row_count]
        )
    return summed


def temporal(series_block):
    frame_total, item_count, columns = series_block.shape
    values = series_block.astype(jnp.float32).reshape(frame_total, item_count * columns)
    frame_ids = jnp.arange(frame_total)
    at_ends = (frame_ids == 0) | (frame_ids == frame_total - 1)
    middle = (1.0 + SMOOTHING * jnp.where(at_ends, 1.0, 2.0)).astype(jnp.float32)
    sub_diag = jnp.where(frame_ids == 0, 0.0, -SMOOTHING).astype(jnp.float32)
    super_diag = jnp.where(frame_ids == frame_total - 1, 0.0, -SMOOTHING).astype(jnp.float32)
    baseline = lax.linalg.tridiagonal_solve(sub_diag, middle, super_diag, values)
    detrended = values - baseline
    earlier = jnp.concatenate(
        [jnp.zeros((1, values.shape[1]), jnp.float32), detrended[:-1]], axis=0
    )
    result = (detrended - DECAY_RATE * earlier).astype(jnp.bfloat16)
    return result.reshape(frame_total, item_count, columns)


def local(observed, kernels, band_kernel, masks):
    frames_dev, rows_dev, row_pixels = observed.shape
    height = rows_dev * lax.axis_size("row")
    tap_table = kernels / jnp.sum(kernels, axis=1, keepdims=True)
    first_row = lax.axis_index("row") * rows_dev
    own_taps = tap_rows(tap_table, band_kernel, first_row, rows_dev, height)
    outer_taps = tap_rows(tap_table, band_kernel, first_row - 2, rows_dev + 4, height)
    current = observed
    for iteration in range(ITERS):
        padded = padded_2(current, (("row", 1),), 2)
        blurred = blur_rows(padded, own_taps, rows_dev)
        quotient = observed / blurred
        padded_quotient = padded_2(quotient, (("row", 1),), 2)
        current = current * back_rows(padded_quotient, outer_taps, rows_dev)
    estimate = current.astype(jnp.bfloat16)
    spikes = temporal(lax.all_to_all(estimate, "frame", split_axis=2, concat_axis=0, tiled=True))
    frames_all, _, columns = spikes.shape
    tile_count = columns // TILE
    tile_sums = jnp.sum(
        spikes.reshape(frames_all, rows_dev * tile_count, TILE).astype(jnp.float32), axis=2
    )
    weights = masks.astype(jnp.float32).reshape(masks.shape[0], rows_dev * tile_count)
    local_sums = lax.dot_general(
        weights, tile_sums, (((1,), (1,)), ((), ())), precision=lax.Precision.HIGHEST
    )
    counts = jnp.sum(weights, axis=1)
    trace_sums, totals = (
        lax.psum_scatter(local_sums, ("frame", "row"), scatter_dimension=0, tiled=True),
        lax.psum_scatter(counts, ("frame", "row"), scatter_dimension=0, tiled=True),
    )
    traces = trace_sums / (TILE * totals[:, None])
    return (spikes, traces)


def solution(mesh):
    in_specs = (
        P("frame", ("groups", "row"), None),
        P(),
        P("groups"),
        P(None, ("groups", "row"), "frame"),
    )
    out_specs = (P(None, ("groups", "row"), "frame"), P(("groups", "frame", "row"), None))
    return jax.shard_map(local, mesh=mesh, in_specs=in_specs, out_specs=out_specs, check_vma=False)
```

profile of v0, /device:TPU:0, one launch (start us, length us, event | category | flops | bytes accessed | tf_op | source)
XLA Modules:
  0.0 222.3 jit_solution(17117470301086755105)
XLA Ops:
  7.2 1.1 fusion.69
  8.4 5.0 %collective-permute-start = (f32[4,2,2048]{2,0,1:T(4,128)S(1)}, f32[4,2,2048]{2,0,1:T(4,128)S(1)}, u32[]{:S(2)}, u32[]{:S(2)}) collective-permute-start(f32[4,2,2048]{2,0,1:T(4,128)S(1)} %copy.150), channel_id=1, source_target_pairs={{0,1},{1,2},{2,3},{4,5},{5,6},{6,7},{8,9},{9,10},{10,11},{12,13},{... | collective-permute-start | bytes 196616 | tf_op jit(solution)/shard_map/ppermute | solution.py:21
  13.4 1.3 collective-permute-start.1
  14.7 0.8 reduce_sum.64
  15.5 0.8 broadcast_divide_fusion.1
  16.3 0.1 copy.106
  16.4 0.7 select_reduce_fusion.2
  17.1 0.1 select_reduce_fusion
  17.2 0.7 select_reduce_fusion.3
  18.0 0.1 select_reduce_fusion.1
  18.1 0.1 slice_bitcast_fusion.24
  18.1 0.9 convert_element_type.45
  19.1 1.5 constant_dynamic-update-slice_fusion
  20.6 0.8 fusion.56
  21.4 1.3 collective-permute-start.2
  22.7 5.2 %collective-permute-start.3 = (f32[4,2,2048]{2,0,1:T(4,128)S(1)}, f32[4,2,2048]{2,0,1:T(4,128)S(1)}, u32[]{:S(2)}, u32[]{:S(2)}) collective-permute-start(f32[4,2,2048]{2,0,1:T(4,128)S(1)} %get-tuple-element.75), channel_id=1, source_target_pairs={{0,1},{1,2},{2,3},{4,5},{5,6},{6,7},{8,9},{9,10},{10,11},{12,13},{... | collective-permute-start | bytes 196616 | tf_op jit(solution)/shard_map/ppermute | solution.py:21
  27.9 0.3 collective-permute-done.2
  28.2 1.6 collective-permute-done.3
  29.8 0.9 fusion.40
  30.7 4.3 %collective-permute-start.4 = (f32[4,2,2048]{2,0,1:T(4,128)S(1)}, f32[4,2,2048]{2,0,1:T(4,128)S(1)}, u32[]{:S(2)}, u32[]{:S(2)}) collective-permute-start(f32[4,2,2048]{2,0,1:T(4,128)S(1)} %get-tuple-element.72), channel_id=1, source_target_pairs={{0,1},{1,2},{2,3},{4,5},{5,6},{6,7},{8,9},{9,10},{10,11},{12,13},{... | collective-permute-start | bytes 196616 | tf_op jit(solution)/shard_map/ppermute | solution.py:21
  34.9 1.3 collective-permute-start.5
  36.2 0.7 fusion.71
  37.0 4.1 %collective-permute-done.5 = f32[4,2,2048]{2,0,1:T(4,128)S(1)} collective-permute-done((f32[4,2,2048]{2,0,1:T(4,128)S(1)}, f32[4,2,2048]{2,0,1:T(4,128)S(1)}, u32[]{:S(2)}, u32[]{:S(2)}) %collective-permute-start.5) | collective-permute-done | bytes 65568 | tf_op jit(solution)/shard_map/ppermute | solution.py:23
  41.1 0.9 fusion.31
  42.0 1.3 collective-permute-start.6
  43.3 4.5 %collective-permute-start.7 = (f32[4,2,2048]{2,0,1:T(4,128)S(1)}, f32[4,2,2048]{2,0,1:T(4,128)S(1)}, u32[]{:S(2)}, u32[]{:S(2)}) collective-permute-start(f32[4,2,2048]{2,0,1:T(4,128)S(1)} %get-tuple-element.71), channel_id=1, source_target_pairs={{0,1},{1,2},{2,3},{4,5},{5,6},{6,7},{8,9},{9,10},{10,11},{12,13},{... | collective-permute-start | bytes 196616 | tf_op jit(solution)/shard_map/ppermute | solution.py:21
  47.9 0.3 collective-permute-done.6
  48.2 1.6 collective-permute-done.7
  49.8 0.6 fusion.22
  50.4 4.3 %collective-permute-start.8 = (f32[4,2,2048]{2,0,1:T(4,128)S(1)}, f32[4,2,2048]{2,0,1:T(4,128)S(1)}, u32[]{:S(2)}, u32[]{:S(2)}) collective-permute-start(f32[4,2,2048]{2,0,1:T(4,128)S(1)} %get-tuple-element.68), channel_id=1, source_target_pairs={{0,1},{1,2},{2,3},{4,5},{5,6},{6,7},{8,9},{9,10},{10,11},{12,13},{... | collective-permute-start | bytes 196616 | tf_op jit(solution)/shard_map/ppermute | solution.py:21
  54.7 1.3 collective-permute-start.9
  56.0 0.7 fusion.72
  58.0 3.5 %collective-permute-done.9 = f32[4,2,2048]{2,0,1:T(4,128)S(1)} collective-permute-done((f32[4,2,2048]{2,0,1:T(4,128)S(1)}, f32[4,2,2048]{2,0,1:T(4,128)S(1)}, u32[]{:S(2)}, u32[]{:S(2)}) %collective-permute-start.9) | collective-permute-done | bytes 65568 | tf_op jit(solution)/shard_map/ppermute | solution.py:23
  61.5 0.9 fusion.13
  62.4 1.3 collective-permute-start.10
  63.7 4.5 %collective-permute-start.11 = (f32[4,2,2048]{2,0,1:T(4,128)S(1)}, f32[4,2,2048]{2,0,1:T(4,128)S(1)}, u32[]{:S(2)}, u32[]{:S(2)}) collective-permute-start(f32[4,2,2048]{2,0,1:T(4,128)S(1)} %get-tuple-element.67), channel_id=1, source_target_pairs={{0,1},{1,2},{2,3},{4,5},{5,6},{6,7},{8,9},{9,10},{10,11},{12,13},{... | collective-permute-start | bytes 196616 | tf_op jit(solution)/shard_map/ppermute | solution.py:21
  68.2 0.3 collective-permute-done.10
  68.5 1.6 collective-permute-done.11
  70.1 0.6 fusion.60
  70.7 1.5 copy.117
  72.2 2.9 %reshape.1472 = bf16[4,2,16384]{2,1,0:T(2,128)(2,1)} reshape(bf16[2048,4,16]{2,1,0:T(4,128)(2,1)S(1)} %bitcast.135) | data formatting | bytes 524288
  75.1 3.4 %all-to-all-start = ((bf16[4,2,16384]{2,1,0:T(2,128)(2,1)}), bf16[4,2,16384]{2,1,0:T(2,128)(2,1)S(1)}, u32[]{:S(2)}, u32[]{:S(2)}) async-start(bf16[4,2,16384]{2,1,0:T(2,128)(2,1)} %reshape.1472), calls=%async_computation | async-start | bytes 524288 | tf_op jit(solution)/shard_map/all_to_all | solution.py:97
  78.6 0.7 fusion.70
  106.8 0.6 dynamic-slice
  108.1 35.6 %all-reduce.1 = f32[256]{0:T(256)S(1)} all-reduce(f32[256]{0:T(256)S(1)} %convert_reduce_fusion), channel_id=3, replica_groups=mesh['groups'=2,'frame'=4,'row'=4] {'frame','row'}, use_global_device_ids=true, to_apply=%region_8.9.clone | all-reduce | flops 256 | bytes 2048
  143.7 1.4 reshape.1473
  145.1 1.1 copy.118
  146.3 0.4 reshape.1467
  146.7 0.2 copy.119
  146.9 0.7 slice_bitcast_fusion
  148.3 0.3 copy.124
  148.6 9.3 %subtract_divide_fusion.1 = (f32[1,8192]{1,0:T(1,128)S(1)}, f32[1,8192]{1,0:T(1,128)S(1)}, f32[1,8192]{1,0:T(1,128)S(1)}, f32[1,8192]{1,0:T(1,128)S(1)}, f32[1,8...) fusion(f32[1,8192]{1,0:T(1,128)S(1)} %bitcast.161, ...), kind=kLoop, calls=%fused_computation.131 | loop fusion | flops 344064 | bytes 950384 | tf_op jit(solution)/shard_map/eval_jaxpr/div | solution.py:73
  157.9 1.0 multiply_subtract_fusion
  158.9 0.8 concatenate.72
  159.7 0.1 convert_bitcast_fusion
  159.8 0.1 copy.142
  159.9 0.2 reduce_sum.68
  160.1 0.1 convolution_bitcast_fusion
  160.3 0.7 copy.122
  161.1 0.1 dynamic-slice_multiply_fusion
  161.1 0.8 copy.141
  161.9 52.1 %reduce-scatter.4.cloned.1.call-done = f32[16,16]{1,0:T(8,128)} async-done(((f32[256,16]{1,0:T(8,128)}), f32[16,16]{1,0:T(8,128)}) %reduce-scatter.4.cloned.1.call-update) | async-done | bytes 1040
  214.0 0.8 copy.123
  214.8 0.7 copy.121
  (50 shorter events, 1.0 us)
Async XLA Ops:
  7.2 13.4 %copy-start = (f32[4,16,2048]{2,1,0:T(8,128)S(1)}, f32[4,16,2048]{2,1,0:T(8,128)}, u32[]{:S(2)}) copy-start(f32[4,16,2048]{2,1,0:T(8,128)} %param.4) | copy-start | bytes 1572868
  8.4 10.7 %collective-permute-start = (f32[4,2,2048]{2,0,1:T(4,128)S(1)}, f32[4,2,2048]{2,0,1:T(4,128)S(1)}, u32[]{:S(2)}, u32[]{:S(2)}) collective-permute-start(f32[4,2,2048]{2,0,1:T(4,128)S(1)} %copy.150), channel_id=1, source_target_pairs={{0,1},{1,2},{2,3},{4,5},{5,6},{6,7},{8,9},{9,10},{10,11},{12,13},{... | collective-permute-start | bytes 196616 | tf_op jit(solution)/shard_map/ppermute | solution.py:21
  13.4 7.2 %collective-permute-start.1 = (f32[4,2,2048]{2,0,1:T(4,128)S(1)}, f32[4,2,2048]{2,0,1:T(4,128)S(1)}, u32[]{:S(2)}, u32[]{:S(2)}) collective-permute-start(f32[4,2,2048]{2,0,1:T(4,128)S(1)} %copy.149), channel_id=1, source_target_pairs={{1,0},{2,1},{3,2},{5,4},{6,5},{7,6},{9,8},{10,9},{11,10},{13,12},{... | collective-permute-start | bytes 196616 | tf_op jit(solution)/shard_map/ppermute | solution.py:23
  21.4 6.8 %collective-permute-start.2 = (f32[4,2,2048]{2,0,1:T(4,128)S(1)}, f32[4,2,2048]{2,0,1:T(4,128)S(1)}, u32[]{:S(2)}, u32[]{:S(2)}) collective-permute-start(f32[4,2,2048]{2,0,1:T(4,128)S(1)} %get-tuple-element.74), channel_id=1, source_target_pairs={{1,0},{2,1},{3,2},{5,4},{6,5},{7,6},{9,8},{10,9},{11,10},{13,12},{... | collective-permute-start | bytes 196616 | tf_op jit(solution)/shard_map/ppermute | solution.py:23
  22.7 7.1 %collective-permute-start.3 = (f32[4,2,2048]{2,0,1:T(4,128)S(1)}, f32[4,2,2048]{2,0,1:T(4,128)S(1)}, u32[]{:S(2)}, u32[]{:S(2)}) collective-permute-start(f32[4,2,2048]{2,0,1:T(4,128)S(1)} %get-tuple-element.75), channel_id=1, source_target_pairs={{0,1},{1,2},{2,3},{4,5},{5,6},{6,7},{8,9},{9,10},{10,11},{12,13},{... | collective-permute-start | bytes 196616 | tf_op jit(solution)/shard_map/ppermute | solution.py:21
  30.7 6.3 %collective-permute-start.4 = (f32[4,2,2048]{2,0,1:T(4,128)S(1)}, f32[4,2,2048]{2,0,1:T(4,128)S(1)}, u32[]{:S(2)}, u32[]{:S(2)}) collective-permute-start(f32[4,2,2048]{2,0,1:T(4,128)S(1)} %get-tuple-element.72), channel_id=1, source_target_pairs={{0,1},{1,2},{2,3},{4,5},{5,6},{6,7},{8,9},{9,10},{10,11},{12,13},{... | collective-permute-start | bytes 196616 | tf_op jit(solution)/shard_map/ppermute | solution.py:21
  34.9 6.2 %collective-permute-start.5 = (f32[4,2,2048]{2,0,1:T(4,128)S(1)}, f32[4,2,2048]{2,0,1:T(4,128)S(1)}, u32[]{:S(2)}, u32[]{:S(2)}) collective-permute-start(f32[4,2,2048]{2,0,1:T(4,128)S(1)} %get-tuple-element.73), channel_id=1, source_target_pairs={{1,0},{2,1},{3,2},{5,4},{6,5},{7,6},{9,8},{10,9},{11,10},{13,12},{... | collective-permute-start | bytes 196616 | tf_op jit(solution)/shard_map/ppermute | solution.py:23
  42.0 6.2 %collective-permute-start.6 = (f32[4,2,2048]{2,0,1:T(4,128)S(1)}, f32[4,2,2048]{2,0,1:T(4,128)S(1)}, u32[]{:S(2)}, u32[]{:S(2)}) collective-permute-start(f32[4,2,2048]{2,0,1:T(4,128)S(1)} %get-tuple-element.70), channel_id=1, source_target_pairs={{1,0},{2,1},{3,2},{5,4},{6,5},{7,6},{9,8},{10,9},{11,10},{13,12},{... | collective-permute-start | bytes 196616 | tf_op jit(solution)/shard_map/ppermute | solution.py:23
  43.3 6.4 %collective-permute-start.7 = (f32[4,2,2048]{2,0,1:T(4,128)S(1)}, f32[4,2,2048]{2,0,1:T(4,128)S(1)}, u32[]{:S(2)}, u32[]{:S(2)}) collective-permute-start(f32[4,2,2048]{2,0,1:T(4,128)S(1)} %get-tuple-element.71), channel_id=1, source_target_pairs={{0,1},{1,2},{2,3},{4,5},{5,6},{6,7},{8,9},{9,10},{10,11},{12,13},{... | collective-permute-start | bytes 196616 | tf_op jit(solution)/shard_map/ppermute | solution.py:21
  50.4 7.6 %collective-permute-start.8 = (f32[4,2,2048]{2,0,1:T(4,128)S(1)}, f32[4,2,2048]{2,0,1:T(4,128)S(1)}, u32[]{:S(2)}, u32[]{:S(2)}) collective-permute-start(f32[4,2,2048]{2,0,1:T(4,128)S(1)} %get-tuple-element.68), channel_id=1, source_target_pairs={{0,1},{1,2},{2,3},{4,5},{5,6},{6,7},{8,9},{9,10},{10,11},{12,13},{... | collective-permute-start | bytes 196616 | tf_op jit(solution)/shard_map/ppermute | solution.py:21
  54.7 6.8 %collective-permute-start.9 = (f32[4,2,2048]{2,0,1:T(4,128)S(1)}, f32[4,2,2048]{2,0,1:T(4,128)S(1)}, u32[]{:S(2)}, u32[]{:S(2)}) collective-permute-start(f32[4,2,2048]{2,0,1:T(4,128)S(1)} %get-tuple-element.69), channel_id=1, source_target_pairs={{1,0},{2,1},{3,2},{5,4},{6,5},{7,6},{9,8},{10,9},{11,10},{13,12},{... | collective-permute-start | bytes 196616 | tf_op jit(solution)/shard_map/ppermute | solution.py:23
  62.4 6.2 %collective-permute-start.10 = (f32[4,2,2048]{2,0,1:T(4,128)S(1)}, f32[4,2,2048]{2,0,1:T(4,128)S(1)}, u32[]{:S(2)}, u32[]{:S(2)}) collective-permute-start(f32[4,2,2048]{2,0,1:T(4,128)S(1)} %get-tuple-element.66), channel_id=1, source_target_pairs={{1,0},{2,1},{3,2},{5,4},{6,5},{7,6},{9,8},{10,9},{11,10},{13,12},{... | collective-permute-start | bytes 196616 | tf_op jit(solution)/shard_map/ppermute | solution.py:23
  63.7 6.4 %collective-permute-start.11 = (f32[4,2,2048]{2,0,1:T(4,128)S(1)}, f32[4,2,2048]{2,0,1:T(4,128)S(1)}, u32[]{:S(2)}, u32[]{:S(2)}) collective-permute-start(f32[4,2,2048]{2,0,1:T(4,128)S(1)} %get-tuple-element.67), channel_id=1, source_target_pairs={{0,1},{1,2},{2,3},{4,5},{5,6},{6,7},{8,9},{9,10},{10,11},{12,13},{... | collective-permute-start | bytes 196616 | tf_op jit(solution)/shard_map/ppermute | solution.py:21
  72.2 34.6 %copy-start.2 = (u32[32]{0:T(128)S(1)}, u32[32]{0:T(128)}, u32[]{:S(2)}) copy-start(u32[32]{0:T(128)} %constant.60) | copy-start | bytes 388
  72.2 35.9 %copy-start.1 = (s32[256,16,4]{0,2,1:T(4,128)S(1)}, s32[256,16,4]{0,2,1:T(4,128)}, u32[]{:S(2)}) copy-start(s32[256,16,4]{0,2,1:T(4,128)} %param.7) | copy-start | bytes 196612
  75.1 68.6 %all-to-all-start = ((bf16[4,2,16384]{2,1,0:T(2,128)(2,1)}), bf16[4,2,16384]{2,1,0:T(2,128)(2,1)S(1)}, u32[]{:S(2)}, u32[]{:S(2)}) async-start(bf16[4,2,16384]{2,1,0:T(2,128)(2,1)} %reshape.1472), calls=%async_computation | async-start | bytes 524288 | tf_op jit(solution)/shard_map/all_to_all | solution.py:97
  78.5 135.5 %reduce-scatter.4.cloned.1.call-start = ((), (), s32[]{:S(2)}) async-start(), calls=%async_computation.2 | async-start | bytes 139264
Sparse Core Ops, SparseCore 0:
  161.2 52.7 reduce-scatter.3
where the time goes:
time: 224 us; the launch traced here: 222 us
  waiting for transfers between devices  65.4 us (29%)
  between operations  44.1 us (20%)
  starting transfers between devices  39 us (17%)
  blocking collectives  35.6 us (16%)
  other arithmetic  20.2 us (9%)
  local copies, waits for them, and re-layouts  18 us (8%)
    unnamed x2, waiting for transfers between devices  52.1 us
    unnamed x1, blocking collectives  35.6 us
    ppermute x6, starting transfers between devices, padded_2(): lax.ppermute(tail, axis, [(i, (i + 1) % count) for i in range(ends)])  27.8 us
    div x1, other arithmetic, temporal(): lax.linalg.tridiagonal_solve(sub_diag, middle, super_diag, values)  9.26 us
    unnamed x34, local copies, waits for them, and re-layouts  8.98 us
    ppermute x6, waiting for transfers between devices, padded_2(): lax.ppermute(head, axis, [((i + 1) % count, i) for i in range(ends)])  8.5 us
    ppermute x6, starting transfers between devices, padded_2(): lax.ppermute(head, axis, [((i + 1) % count, i) for i in range(ends)])  7.75 us
    ppermute x6, waiting for transfers between devices, padded_2(): lax.ppermute(tail, axis, [(i, (i + 1) % count) for i in range(ends)])  4.75 us
  transfers between devices with their start and end apart: 14, of which 9 were waited for; matrix products, arithmetic and copies ran while one was open for 4% of the time, Pallas kernels for 0%

commit v1 on v0

--- a/solution.py
+++ b/solution.py
@@ -94,7 +94,14 @@
         padded_quotient = padded_2(quotient, (("row", 1),), 2)
         current = current * back_rows(padded_quotient, outer_taps, rows_dev)
     estimate = current.astype(jnp.bfloat16)
-    spikes = temporal(lax.all_to_all(estimate, "frame", split_axis=2, concat_axis=0, tiled=True))
+    spikes = temporal(
+        jnp.concatenate(
+            lax.all_to_all(
+                jnp.stack(jnp.split(estimate, lax.axis_size("frame"), axis=2)), "frame", 0, 0
+            ),
+            axis=0,
+        )
+    )
     frames_all, _, columns = spikes.shape
     tile_count = columns // TILE
     tile_sums = jnp.sum(

time: 224 us -> 213 us (0.951)
  waiting for transfers between devices: 65.4 us -> 72.8 us
  local copies, waits for them, and re-layouts: 18 us -> 10.8 us
  other arithmetic: 20.2 us -> 15.3 us
  blocking collectives: 35.6 us -> 31.2 us
    ppermute x6, waiting for transfers between devices: 8.5 us -> 16.3 us  [padded_2(): lax.ppermute(head, axis, [((i + 1) % count, i) for i in range(ends)])]
    unnamed x1, blocking collectives: 35.6 us -> 31.2 us
    unnamed x34, local copies, waits for them, and re-layouts: 8.98 us -> 6.32 us
  transfers between devices with their start and end apart: 14 -> 14, of which waited for: 9 -> 9; matrix products, arithmetic and copies ran while one was open for 4% -> 3% of each run, Pallas kernels for 0% -> 0%
where the time goes in v1:
time: 213 us; the launch traced here: 212 us
  waiting for transfers between devices  72.8 us (34%)
  between operations  44 us (21%)
  starting transfers between devices  37.3 us (18%)
  blocking collectives  31.2 us (15%)
  other arithmetic  15.3 us (7%)
  local copies, waits for them, and re-layouts  10.8 us (5%)
    unnamed x2, waiting for transfers between devices  53.6 us
    unnamed x1, blocking collectives  31.2 us
    ppermute x6, starting transfers between devices, padded_2(): lax.ppermute(tail, axis, [(i, (i + 1) % count) for i in range(ends)])  25.9 us
    ppermute x6, waiting for transfers between devices, padded_2(): lax.ppermute(head, axis, [((i + 1) % count, i) for i in range(ends)])  16.3 us
    div x1, other arithmetic, temporal(): lax.linalg.tridiagonal_solve(sub_diag, middle, super_diag, values)  9.24 us
    ppermute x6, starting transfers between devices, padded_2(): lax.ppermute(head, axis, [((i + 1) % count, i) for i in range(ends)])  7.88 us
    unnamed x34, local copies, waits for them, and re-layouts  6.32 us
  transfers between devices with their start and end apart: 14, of which 9 were waited for; matrix products, arithmetic and copies ran while one was open for 3% of the time, Pallas kernels for 0%

profile of v1, /device:TPU:0, one launch (start us, length us, event | category | flops | bytes accessed | tf_op | source)
XLA Modules:
  0.0 211.6 jit_solution(723358336214308564)
XLA Ops:
  7.2 1.1 fusion.72
  8.2 5.0 %collective-permute-start = (f32[4,2,2048]{2,1,0:T(2,128)S(1)}, f32[4,2,2048]{2,1,0:T(2,128)S(1)}, u32[]{:S(2)}, u32[]{:S(2)}) collective-permute-start(f32[4,2,2048]{2,1,0:T(2,128)S(1)} %get-tuple-element.67), channel_id=1, source_target_pairs={{0,1},{1,2},{2,3},{4,5},{5,6},{6,7},{8,9},{9,10},{10,11},{12,13},{... | collective-permute-start | bytes 196616 | tf_op jit(solution)/shard_map/ppermute | solution.py:21
  13.2 1.4 collective-permute-start.1
  14.7 1.1 constant_dynamic-update-slice_fusion.1
  15.8 0.1 reduce_sum.64
  15.9 0.1 broadcast_divide_fusion.1
  16.0 0.1 copy.8
  16.1 0.1 select_reduce_fusion.2
  16.2 0.1 select_reduce_fusion
  16.3 0.1 select_reduce_fusion.3
  16.4 0.1 select_reduce_fusion.1
  16.5 0.1 slice_bitcast_fusion.28
  16.6 0.0 copy-done.1
  16.7 2.9 %collective-permute-done.1 = f32[4,2,2048]{2,1,0:T(2,128)S(1)} collective-permute-done((f32[4,2,2048]{2,1,0:T(2,128)S(1)}, f32[4,2,2048]{2,1,0:T(2,128)S(1)}, u32[]{:S(2)}, u32[]{:S(2)}) %collective-permute-start.1) | collective-permute-done | bytes 65568 | tf_op jit(solution)/shard_map/ppermute | solution.py:23
  19.6 0.4 fusion.52
  20.0 3.5 %collective-permute-start.3 = (f32[4,2,2048]{2,1,0:T(2,128)S(1)}, f32[4,2,2048]{2,1,0:T(2,128)S(1)}, u32[]{:S(2)}, u32[]{:S(2)}) collective-permute-start(f32[4,2,2048]{2,1,0:T(2,128)S(1)} %get-tuple-element.65), channel_id=1, source_target_pairs={{0,1},{1,2},{2,3},{4,5},{5,6},{6,7},{8,9},{9,10},{10,11},{12,13},{... | collective-permute-start | bytes 196616 | tf_op jit(solution)/shard_map/ppermute | solution.py:21
  23.5 1.3 collective-permute-start.2
  24.8 0.6 collective-permute-done.3
  25.4 4.3 %collective-permute-done.2 = f32[4,2,2048]{2,1,0:T(2,128)S(1)} collective-permute-done((f32[4,2,2048]{2,1,0:T(2,128)S(1)}, f32[4,2,2048]{2,1,0:T(2,128)S(1)}, u32[]{:S(2)}, u32[]{:S(2)}) %collective-permute-start.2) | collective-permute-done | bytes 65568 | tf_op jit(solution)/shard_map/ppermute | solution.py:23
  29.7 0.4 fusion.41
  30.2 1.3 collective-permute-start.5
  31.5 4.5 %collective-permute-start.4 = (f32[4,2,2048]{2,1,0:T(2,128)S(1)}, f32[4,2,2048]{2,1,0:T(2,128)S(1)}, u32[]{:S(2)}, u32[]{:S(2)}) collective-permute-start(f32[4,2,2048]{2,1,0:T(2,128)S(1)} %get-tuple-element.62), channel_id=1, source_target_pairs={{0,1},{1,2},{2,3},{4,5},{5,6},{6,7},{8,9},{9,10},{10,11},{12,13},{... | collective-permute-start | bytes 196616 | tf_op jit(solution)/shard_map/ppermute | solution.py:21
  36.0 0.7 fusion.74
  36.8 1.2 collective-permute-done.4
  37.9 0.5 fusion.32
  38.4 4.3 %collective-permute-start.7 = (f32[4,2,2048]{2,1,0:T(2,128)S(1)}, f32[4,2,2048]{2,1,0:T(2,128)S(1)}, u32[]{:S(2)}, u32[]{:S(2)}) collective-permute-start(f32[4,2,2048]{2,1,0:T(2,128)S(1)} %get-tuple-element.61), channel_id=1, source_target_pairs={{0,1},{1,2},{2,3},{4,5},{5,6},{6,7},{8,9},{9,10},{10,11},{12,13},{... | collective-permute-start | bytes 196616 | tf_op jit(solution)/shard_map/ppermute | solution.py:21
  42.7 1.3 collective-permute-start.6
  44.0 0.6 collective-permute-done.7
  44.6 4.9 %collective-permute-done.6 = f32[4,2,2048]{2,1,0:T(2,128)S(1)} collective-permute-done((f32[4,2,2048]{2,1,0:T(2,128)S(1)}, f32[4,2,2048]{2,1,0:T(2,128)S(1)}, u32[]{:S(2)}, u32[]{:S(2)}) %collective-permute-start.6) | collective-permute-done | bytes 65568 | tf_op jit(solution)/shard_map/ppermute | solution.py:23
  49.5 0.4 fusion.23
  50.0 1.3 collective-permute-start.9
  51.3 4.5 %collective-permute-start.8 = (f32[4,2,2048]{2,1,0:T(2,128)S(1)}, f32[4,2,2048]{2,1,0:T(2,128)S(1)}, u32[]{:S(2)}, u32[]{:S(2)}) collective-permute-start(f32[4,2,2048]{2,1,0:T(2,128)S(1)} %get-tuple-element.58), channel_id=1, source_target_pairs={{0,1},{1,2},{2,3},{4,5},{5,6},{6,7},{8,9},{9,10},{10,11},{12,13},{... | collective-permute-start | bytes 196616 | tf_op jit(solution)/shard_map/ppermute | solution.py:21
  55.8 0.7 fusion.75
  57.9 0.4 fusion.14
  58.4 4.1 %collective-permute-start.11 = (f32[4,2,2048]{2,1,0:T(2,128)S(1)}, f32[4,2,2048]{2,1,0:T(2,128)S(1)}, u32[]{:S(2)}, u32[]{:S(2)}) collective-permute-start(f32[4,2,2048]{2,1,0:T(2,128)S(1)} %get-tuple-element.57), channel_id=1, source_target_pairs={{0,1},{1,2},{2,3},{4,5},{5,6},{6,7},{8,9},{9,10},{10,11},{12,13},{... | collective-permute-start | bytes 196616 | tf_op jit(solution)/shard_map/ppermute | solution.py:21
  62.5 1.3 collective-permute-start.10
  63.8 0.6 collective-permute-done.11
  64.4 4.3 %collective-permute-done.10 = f32[4,2,2048]{2,1,0:T(2,128)S(1)} collective-permute-done((f32[4,2,2048]{2,1,0:T(2,128)S(1)}, f32[4,2,2048]{2,1,0:T(2,128)S(1)}, u32[]{:S(2)}, u32[]{:S(2)}) %collective-permute-start.10) | collective-permute-done | bytes 65568 | tf_op jit(solution)/shard_map/ppermute | solution.py:23
  68.7 0.4 fusion.5
  69.1 0.7 pad_maximum_fusion.11
  69.9 3.4 %all-to-all-start = ((bf16[4,4,16,512]{3,2,1,0:T(8,128)(2,1)}), bf16[4,4,16,512]{3,2,1,0:T(8,128)(2,1)S(1)}, u32[]{:S(2)}, u32[]{:S(2)}) async-start(bf16[4,4,16,512]{3,2,1,0:T(8,128)(2,1)} %pad_maximum_fusion.11), calls=%async_computation | async-start | bytes 524288 | tf_op jit(solution)/shard_map/all_to_all | solution.py:99
  73.3 0.0 reduce-scatter.4.cloned.1.call-start
  73.3 0.7 fusion.73
  101.6 0.6 copy-done.4
  102.2 0.6 dynamic-slice
  103.5 31.2 %all-reduce.1 = f32[256]{0:T(256)S(1)} all-reduce(f32[256]{0:T(256)S(1)} %convert_reduce_fusion), channel_id=3, replica_groups=mesh['groups'=2,'frame'=4,'row'=4] {'frame','row'}, use_global_device_ids=true, to_apply=%region_8.9.clone | all-reduce | flops 256 | bytes 2048
  134.7 0.1 convert_element_type.36
  134.8 0.3 copy.13
  135.1 0.7 slice_bitcast_fusion.4
  136.4 9.2 %subtract_divide_fusion.1 = (f32[1,8192]{1,0:T(1,128)S(1)}, f32[1,8192]{1,0:T(1,128)S(1)}, f32[1,8192]{1,0:T(1,128)S(1)}, f32[1,8192]{1,0:T(1,128)S(1)}, f32[1,8...) fusion(f32[1,8192]{1,0:T(1,128)S(1)} %bitcast.150, ...), kind=kLoop, calls=%fused_computation.140 | loop fusion | flops 344064 | bytes 950384 | tf_op jit(solution)/shard_map/eval_jaxpr/div | solution.py:73
  145.7 0.9 multiply_subtract_fusion
  146.6 0.8 concatenate.72
  147.4 0.1 sub.1744
  147.5 0.1 convert_bitcast_fusion
  147.6 0.1 copy.31
  147.7 0.2 reduce_sum.68
  147.9 0.1 convolution_bitcast_fusion
  148.1 0.7 copy.11
  148.8 0.0 reduce-scatter.4.cloned.1.call-update
  148.8 0.1 dynamic-slice_multiply_fusion
  148.9 0.8 copy.30
  149.7 53.6 %reduce-scatter.4.cloned.1.call-done = f32[16,16]{1,0:T(8,128)} async-done(((f32[256,16]{1,0:T(8,128)}), f32[16,16]{1,0:T(8,128)}) %reduce-scatter.4.cloned.1.call-update) | async-done | bytes 1040
  203.3 0.8 copy.12
  204.1 0.7 copy.10
  (48 shorter events, 1.0 us)
Async XLA Ops:
  8.2 11.3 %collective-permute-start = (f32[4,2,2048]{2,1,0:T(2,128)S(1)}, f32[4,2,2048]{2,1,0:T(2,128)S(1)}, u32[]{:S(2)}, u32[]{:S(2)}) collective-permute-start(f32[4,2,2048]{2,1,0:T(2,128)S(1)} %get-tuple-element.67), channel_id=1, source_target_pairs={{0,1},{1,2},{2,3},{4,5},{5,6},{6,7},{8,9},{9,10},{10,11},{12,13},{... | collective-permute-start | bytes 196616 | tf_op jit(solution)/shard_map/ppermute | solution.py:21
  13.2 6.3 %copy-start = (f32[4,16,2048]{2,1,0:T(8,128)S(1)}, f32[4,16,2048]{2,1,0:T(8,128)}, u32[]{:S(2)}) copy-start(f32[4,16,2048]{2,1,0:T(8,128)} %param.4) | copy-start | bytes 1572868
  13.2 6.3 %collective-permute-start.1 = (f32[4,2,2048]{2,1,0:T(2,128)S(1)}, f32[4,2,2048]{2,1,0:T(2,128)S(1)}, u32[]{:S(2)}, u32[]{:S(2)}) collective-permute-start(f32[4,2,2048]{2,1,0:T(2,128)S(1)} %get-tuple-element.66), channel_id=1, source_target_pairs={{1,0},{2,1},{3,2},{5,4},{6,5},{7,6},{9,8},{10,9},{11,10},{13,12},{... | collective-permute-start | bytes 196616 | tf_op jit(solution)/shard_map/ppermute | solution.py:23
  14.7 1.1 copy-start.2
  14.7 1.4 copy-start.3
  15.8 0.8 copy-start.1
  20.0 5.4 %collective-permute-start.3 = (f32[4,2,2048]{2,1,0:T(2,128)S(1)}, f32[4,2,2048]{2,1,0:T(2,128)S(1)}, u32[]{:S(2)}, u32[]{:S(2)}) collective-permute-start(f32[4,2,2048]{2,1,0:T(2,128)S(1)} %get-tuple-element.65), channel_id=1, source_target_pairs={{0,1},{1,2},{2,3},{4,5},{5,6},{6,7},{8,9},{9,10},{10,11},{12,13},{... | collective-permute-start | bytes 196616 | tf_op jit(solution)/shard_map/ppermute | solution.py:21
  23.5 6.2 %collective-permute-start.2 = (f32[4,2,2048]{2,1,0:T(2,128)S(1)}, f32[4,2,2048]{2,1,0:T(2,128)S(1)}, u32[]{:S(2)}, u32[]{:S(2)}) collective-permute-start(f32[4,2,2048]{2,1,0:T(2,128)S(1)} %get-tuple-element.64), channel_id=1, source_target_pairs={{1,0},{2,1},{3,2},{5,4},{6,5},{7,6},{9,8},{10,9},{11,10},{13,12},{... | collective-permute-start | bytes 196616 | tf_op jit(solution)/shard_map/ppermute | solution.py:23
  30.2 6.6 %collective-permute-start.5 = (f32[4,2,2048]{2,1,0:T(2,128)S(1)}, f32[4,2,2048]{2,1,0:T(2,128)S(1)}, u32[]{:S(2)}, u32[]{:S(2)}) collective-permute-start(f32[4,2,2048]{2,1,0:T(2,128)S(1)} %get-tuple-element.63), channel_id=1, source_target_pairs={{1,0},{2,1},{3,2},{5,4},{6,5},{7,6},{9,8},{10,9},{11,10},{13,12},{... | collective-permute-start | bytes 196616 | tf_op jit(solution)/shard_map/ppermute | solution.py:23
  31.5 6.4 %collective-permute-start.4 = (f32[4,2,2048]{2,1,0:T(2,128)S(1)}, f32[4,2,2048]{2,1,0:T(2,128)S(1)}, u32[]{:S(2)}, u32[]{:S(2)}) collective-permute-start(f32[4,2,2048]{2,1,0:T(2,128)S(1)} %get-tuple-element.62), channel_id=1, source_target_pairs={{0,1},{1,2},{2,3},{4,5},{5,6},{6,7},{8,9},{9,10},{10,11},{12,13},{... | collective-permute-start | bytes 196616 | tf_op jit(solution)/shard_map/ppermute | solution.py:21
  38.4 6.2 %collective-permute-start.7 = (f32[4,2,2048]{2,1,0:T(2,128)S(1)}, f32[4,2,2048]{2,1,0:T(2,128)S(1)}, u32[]{:S(2)}, u32[]{:S(2)}) collective-permute-start(f32[4,2,2048]{2,1,0:T(2,128)S(1)} %get-tuple-element.61), channel_id=1, source_target_pairs={{0,1},{1,2},{2,3},{4,5},{5,6},{6,7},{8,9},{9,10},{10,11},{12,13},{... | collective-permute-start | bytes 196616 | tf_op jit(solution)/shard_map/ppermute | solution.py:21
  42.7 6.8 %collective-permute-start.6 = (f32[4,2,2048]{2,1,0:T(2,128)S(1)}, f32[4,2,2048]{2,1,0:T(2,128)S(1)}, u32[]{:S(2)}, u32[]{:S(2)}) collective-permute-start(f32[4,2,2048]{2,1,0:T(2,128)S(1)} %get-tuple-element.60), channel_id=1, source_target_pairs={{1,0},{2,1},{3,2},{5,4},{6,5},{7,6},{9,8},{10,9},{11,10},{13,12},{... | collective-permute-start | bytes 196616 | tf_op jit(solution)/shard_map/ppermute | solution.py:23
  50.0 7.9 %collective-permute-start.9 = (f32[4,2,2048]{2,1,0:T(2,128)S(1)}, f32[4,2,2048]{2,1,0:T(2,128)S(1)}, u32[]{:S(2)}, u32[]{:S(2)}) collective-permute-start(f32[4,2,2048]{2,1,0:T(2,128)S(1)} %get-tuple-element.59), channel_id=1, source_target_pairs={{1,0},{2,1},{3,2},{5,4},{6,5},{7,6},{9,8},{10,9},{11,10},{13,12},{... | collective-permute-start | bytes 196616 | tf_op jit(solution)/shard_map/ppermute | solution.py:23
  51.3 6.6 %collective-permute-start.8 = (f32[4,2,2048]{2,1,0:T(2,128)S(1)}, f32[4,2,2048]{2,1,0:T(2,128)S(1)}, u32[]{:S(2)}, u32[]{:S(2)}) collective-permute-start(f32[4,2,2048]{2,1,0:T(2,128)S(1)} %get-tuple-element.58), channel_id=1, source_target_pairs={{0,1},{1,2},{2,3},{4,5},{5,6},{6,7},{8,9},{9,10},{10,11},{12,13},{... | collective-permute-start | bytes 196616 | tf_op jit(solution)/shard_map/ppermute | solution.py:21
  58.4 6.0 %collective-permute-start.11 = (f32[4,2,2048]{2,1,0:T(2,128)S(1)}, f32[4,2,2048]{2,1,0:T(2,128)S(1)}, u32[]{:S(2)}, u32[]{:S(2)}) collective-permute-start(f32[4,2,2048]{2,1,0:T(2,128)S(1)} %get-tuple-element.57), channel_id=1, source_target_pairs={{0,1},{1,2},{2,3},{4,5},{5,6},{6,7},{8,9},{9,10},{10,11},{12,13},{... | collective-permute-start | bytes 196616 | tf_op jit(solution)/shard_map/ppermute | solution.py:21
  62.5 6.2 %collective-permute-start.10 = (f32[4,2,2048]{2,1,0:T(2,128)S(1)}, f32[4,2,2048]{2,1,0:T(2,128)S(1)}, u32[]{:S(2)}, u32[]{:S(2)}) collective-permute-start(f32[4,2,2048]{2,1,0:T(2,128)S(1)} %get-tuple-element.56), channel_id=1, source_target_pairs={{1,0},{2,1},{3,2},{5,4},{6,5},{7,6},{9,8},{10,9},{11,10},{13,12},{... | collective-permute-start | bytes 196616 | tf_op jit(solution)/shard_map/ppermute | solution.py:23
  69.9 64.8 %all-to-all-start = ((bf16[4,4,16,512]{3,2,1,0:T(8,128)(2,1)}), bf16[4,4,16,512]{3,2,1,0:T(8,128)(2,1)S(1)}, u32[]{:S(2)}, u32[]{:S(2)}) async-start(bf16[4,4,16,512]{3,2,1,0:T(8,128)(2,1)} %pad_maximum_fusion.11), calls=%async_computation | async-start | bytes 524288 | tf_op jit(solution)/shard_map/all_to_all | solution.py:99
  73.3 130.0 %reduce-scatter.4.cloned.1.call-start = ((), (), s32[]{:S(2)}) async-start(), calls=%async_computation.2 | async-start | bytes 139264
  101.5 0.7 copy-start.4
Sparse Core Ops, SparseCore 0:
  148.9 54.3 reduce-scatter.3
